TPU v7x, 32 devices: a whole 2x2x4 slice. The times are simulated.
32 devices in a mesh: dp: 8 (over y, x, core), span: 4 (over z).
Axes of the slice: x: 2, y: 2, z: 4, core: 2. Of those that a mesh axis runs over, the one named last changes fastest.
Arguments:
- features: bfloat16 [8, 1024, 1024], P('dp', 'span'), may hold values from -6 to 6
- lengths: int32 [8], P('dp'), may hold values from 256 to 1024, as said below
- labels: int32 [8, 1024], P('dp', 'span'), may hold values from 0 to 4
- w_first: bfloat16 [1024, 1024], replicated, may hold values from -0.1875 to 0.1875
- b_first: float32 [1024], replicated, may hold values from -3 to 3
- w_second: bfloat16 [1024, 256], replicated, may hold values from -0.375 to 0.375
Outputs:
- loss: float32 [], replicated
- grad_first: float32 [1024, 1024], replicated
- grad_bias: float32 [1024], replicated
- grad_second: float32 [1024, 256], replicated
Inputs may be any that keep to these rules, and one draw needn't show every extreme that they name: `lengths`: every list has 256 or more real candidates, and some list has exactly 1024.
All inputs are finite; a program needn't handle non-finite values.
Results may differ from a plain program's by a relative error of at most 0.004.
Values may be sent and summed in bfloat16 or wider, within the bound.
A program may use at most 64 MiB of HBM per device.

v0:
```python
import math

import jax
import jax.numpy as jnp
from jax import lax
from jax.sharding import PartitionSpec as P

gain_values = (0.0, 1.0, 3.0, 7.0, 15.0)
log_two = math.log(2.0)


def level_onehot(labels):
    return (labels[..., None] == jnp.arange(5, dtype=jnp.int32)).astype(jnp.float32)


def ideal_gain(level_counts, list_len):
    levels = jnp.arange(5, dtype=jnp.int32)
    above_mask = (levels[:, None] > levels[None, :]).astype(jnp.float32)
    starts = jnp.sum(level_counts[:, None] * above_mask, axis=0)
    finish = starts + level_counts
    places = jnp.arange(1, list_len + 1, dtype=jnp.int32).astype(jnp.float32)
    discount = log_two / jnp.log1p(places)
    inside = (places[None, :] > starts[:, None]) & (places[None, :] <= finish[:, None])
    per_level = jnp.sum(jnp.where(inside, discount[None, :], 0.0), axis=1)
    return jnp.maximum(jnp.sum(per_level * jnp.asarray(gain_values, jnp.float32)), 1.0)


def rank_part(row_emb, block_keys, block_mask, pair_scale):
    logits = (
        jnp.einsum("ik,jk->ij", row_emb, block_keys, preferred_element_type=jnp.float32)
        * pair_scale
    )
    return jnp.sum(jax.nn.sigmoid(-logits) * block_mask.astype(jnp.float32)[None, :], axis=1)


def grad_part(row_emb, row_weight, row_mask, block_keys, key_weight, key_mask, pair_scale):
    logits = (
        jnp.einsum("ik,jk->ij", row_emb, block_keys, preferred_element_type=jnp.float32)
        * pair_scale
    )
    probab = jax.nn.sigmoid(logits)
    pair_grad = (
        probab
        * (1.0 - probab)
        * (row_mask[:, None] * key_weight[None, :] - row_weight[:, None] * key_mask[None, :])
    )
    return (
        jnp.dot(pair_grad.astype(jnp.bfloat16), block_keys, preferred_element_type=jnp.float32)
        * pair_scale
    )


def shards(features, lengths, labels, w_first, b_first, w_second):
    row_feats = features[0]
    row_count = row_feats.shape[0]
    half_width = w_second.shape[1] // 2
    pair_scale = 1.0 / math.sqrt(half_width)
    span_count = lax.axis_size("span")
    list_count = lax.axis_size("dp")
    list_len = row_count * span_count
    row_start = lax.axis_index("span") * row_count
    length = lengths[0]
    in_list = (row_start + jnp.arange(row_count, dtype=jnp.int32) < length).astype(jnp.float32)
    onehot = level_onehot(labels[0]) * in_list[:, None]
    gain_row = jnp.sum(onehot * jnp.asarray(gain_values, jnp.float32)[None, :], axis=1)
    level_counts = lax.psum(jnp.sum(onehot, axis=0), "span")
    ideal = ideal_gain(level_counts, list_len)
    pre_act = jnp.dot(row_feats, w_first, preferred_element_type=jnp.float32) + b_first[None, :]
    hidden = jnp.maximum(pre_act, 0.0).astype(jnp.bfloat16)
    row_emb = jnp.dot(hidden, w_second, preferred_element_type=jnp.float32).astype(jnp.bfloat16)
    key_rows = jnp.concatenate([row_emb[:, half_width:], -row_emb[:, :half_width]], axis=1)
    mask_half = in_list.astype(jnp.bfloat16)
    result = rank_part(
        row_emb,
        lax.all_gather(key_rows, "span", axis=0, tiled=True),
        lax.all_gather(mask_half, "span", axis=0, tiled=True),
        pair_scale,
    )
    rank_sum = result
    soft_rank = 0.5 + rank_sum
    log_rank = jnp.log1p(soft_rank)
    approx_dcg = jnp.sum(gain_row * log_two / log_rank)
    loss_part = (1.0 / span_count - approx_dcg / ideal) / list_count
    row_weight = (
        gain_row / (ideal * list_count) * log_two / ((1.0 + soft_rank) * log_rank * log_rank)
    )
    all_weight, all_live = (
        lax.all_gather(row_weight, "span", axis=0, tiled=True),
        lax.all_gather(in_list, "span", axis=0, tiled=True),
    )
    result = grad_part(
        row_emb,
        row_weight,
        in_list,
        lax.all_gather(key_rows, "span", axis=0, tiled=True),
        all_weight,
        all_live,
        pair_scale,
    )
    grad_emb = result.astype(jnp.bfloat16)
    grad_second = jnp.einsum("ch,ce->he", hidden, grad_emb, preferred_element_type=jnp.float32)
    back_hidden = jnp.einsum("ce,he->ch", grad_emb, w_second, preferred_element_type=jnp.float32)
    grad_pre = jnp.where(pre_act > 0.0, back_hidden, 0.0).astype(jnp.bfloat16)
    grad_bias = jnp.sum(grad_pre.astype(jnp.float32), axis=0)
    grad_first = jnp.einsum("cd,ch->dh", row_feats, grad_pre, preferred_element_type=jnp.float32)
    total_first, total_bias, total_second, loss = lax.psum(
        (grad_first, grad_bias, grad_second, loss_part), ("dp", "span")
    )
    return (loss, total_first, total_bias, total_second)


def solution(mesh):
    placed = (P("dp", "span", None), P("dp"), P("dp", "span"), P(), P(), P())
    return jax.shard_map(
        shards, mesh=mesh, in_specs=placed, out_specs=(P(), P(), P(), P()), check_vma=False
    )
```

profile of v0, /device:TPU:0, one launch (start us, length us, event | category | flops | bytes accessed | tf_op | source)
XLA Modules:
  0.0 237.0 jit_solution(1762911410404835875)
XLA Ops:
  7.2 0.0 copy-start
  7.2 0.0 all-reduce.4.cloned.1.call-start
  8.1 0.9 select_reduce_fusion.1
  9.0 13.5 %psum.35 = f32[5]{0:T(128)S(1)} all-reduce(f32[5]{0:T(128)S(1)} %get-tuple-element.16), channel_id=1, replica_groups=mesh['dp'=8,'span'=4] {'span'}, use_global_device_ids=true, to_apply=%region_4.5 | all-reduce | flops 5 | bytes 40 | tf_op jit(solution)/shard_map/psum | solution.py:66
  22.4 0.0 copy-start.1
  22.4 0.1 select_reduce_fusion.2
  22.5 7.7 %all-gather = bf16[4,1,256]{2,1,0:T(2,128)(2,1)S(1)} all-gather(bf16[1,1,256]{2,1,0:T(2,128)(2,1)S(1)} %reshape.44), channel_id=1, replica_groups=mesh['dp'=8,'span'=4] {'span'}, dimensions={0}, use_global_device_ids=true | all-gather | bytes 2560 | tf_op jit(solution)/shard_map/all_gather | solution.py:76
  30.2 9.6 %all-gather.2 = f32[4,1,256]{2,1,0:T(1,128)S(1)} all-gather(f32[1,1,256]{2,1,0:T(1,128)S(1)} %bitcast.25), channel_id=1, replica_groups=mesh['dp'=8,'span'=4] {'span'}, dimensions={0}, use_global_device_ids=true | all-gather | bytes 5120 | tf_op jit(solution)/shard_map/all_gather | solution.py:89
  39.8 0.2 select_reduce_fusion
  40.0 1.3 multiply_reduce_fusion.1
  41.3 0.0 copy-done
  41.3 1.8 convolution_add_fusion
  43.0 0.0 copy-done.1
  43.1 0.4 convolution_convert_fusion
  43.4 16.3 %all_gather.13 = bf16[1024,256]{0,1:T(8,128)(2,1)} all-gather(bf16[256,256]{0,1:T(8,128)(2,1)S(1)} %pad_maximum_fusion), channel_id=1, replica_groups=mesh['dp'=8,'span'=4] {'span'}, dimensions={0}, use_global_device_ids=true | all-gather | bytes 655360 | tf_op jit(solution)/shard_map/all_gather | solution.py:75
  60.4 0.0 copy-start.5
  60.4 1.7 multiply_reduce_fusion
  62.0 0.0 copy-start.2
  62.1 0.6 fusion.9
  62.7 8.0 %all-gather.1 = f32[4,1,256]{2,1,0:T(1,128)S(1)} all-gather(f32[1,1,256]{2,1,0:T(1,128)S(1)} %bitcast.29), channel_id=1, replica_groups=mesh['dp'=8,'span'=4] {'span'}, dimensions={0}, use_global_device_ids=true | all-gather | bytes 5120 | tf_op jit(solution)/shard_map/all_gather | solution.py:88
  70.7 0.0 copy-done.5
  70.7 0.0 copy-start.4
  70.7 0.5 fusion.1
  71.2 0.0 copy-done.2
  71.2 0.3 convert_reduce_fusion
  71.6 1.3 fusion.7
  72.9 0.0 copy-done.4
  72.9 2.8 %convolution_bitcast_fusion = f32[1024,1024]{0,1:T(8,128)} fusion(bf16[256,1024]{1,0:T(8,128)(2,1)S(1)} %get-tuple-element.29, bf16[1,256,1024]{2,1,0:T(8,128)(2,1)S(1)} %copy-done.4), kind=kOutput, calls=%fused_computation | convolution fusion | flops 536870912 | bytes 5242880 | tf_op jit(solution)/shard_map/cd,ch->dh/dot_general | solution.py:105
  75.7 0.0 all-reduce.4.cloned.1.call-update
  76.3 40.8 %all-reduce = (f32[]{:T(128)}, f32[1024]{0:T(1024)}) all-reduce(f32[]{:T(128)S(6)} %div.47, f32[1024]{0:T(1024)S(1)} %get-tuple-element.28), channel_id=1, replica_groups=mesh['dp'=8,'span'=4] {'dp','span'}, use_global_device_ids=true, to_apply=%region_8.9 | all-reduce | flops 1025 | bytes 8200 | tf_op jit(solution)/shard_map/psum | solution.py:106
  117.2 106.5 %all-reduce.4.cloned.1.call-done = (f32[1024,1024]{0,1:T(8,128)}, f32[1024,256]{1,0:T(8,128)}) async-done(((f32[1024,1024]{0,1:T(8,128)}, f32[1024,256]{1,0:T(8,128)}), (f32[1024,1024]{0,1:T(8,128)}, f32[1024,256]{1,0:T(8,128)})) %all-reduce.4.cloned.1.call-update) | async-done | bytes 5242896 | tf_op jit(solution)/shard_map/psum | solution.py:106
  223.7 0.0 copy-start.3
  223.7 5.4 %copy.14 = f32[1024,1024]{1,0:T(8,128)} copy(f32[1024,1024]{0,1:T(8,128)} %get-tuple-element.20) | data formatting | bytes 8388608
  229.1 0.0 copy-done.3
  229.2 1.0 copy.18
  (9 shorter events, 0.1 us)
Async XLA Ops:
  7.2 34.1 %copy-start = (bf16[1024,1024]{1,0:T(8,128)(2,1)S(1)}, bf16[1024,1024]{1,0:T(8,128)(2,1)}, u32[]{:S(2)}) copy-start(bf16[1024,1024]{1,0:T(8,128)(2,1)} %param.11) | copy-start | bytes 6291460
  7.2 216.5 %all-reduce.4.cloned.1.call-start = ((), (), s32[]{:S(2)}) async-start(), calls=%async_computation | async-start | bytes 10485760 | tf_op jit(solution)/shard_map/psum | solution.py:106
  22.4 20.6 %copy-start.1 = (bf16[1024,256]{1,0:T(8,128)(2,1)S(1)}, bf16[1024,256]{1,0:T(8,128)(2,1)}, u32[]{:S(2)}) copy-start(bf16[1024,256]{1,0:T(8,128)(2,1)} %param.13) | copy-start | bytes 1572868
  60.4 10.3 %copy-start.5 = (bf16[1024,256]{0,1:T(8,128)(2,1)S(1)}, bf16[1024,256]{0,1:T(8,128)(2,1)}, u32[]{:S(2)}) copy-start(bf16[1024,256]{0,1:T(8,128)(2,1)} %all_gather.13) | copy-start | bytes 1572868
  62.0 9.2 %copy-start.2 = (bf16[1024,256]{1,0:T(8,128)(2,1)S(1)}, bf16[1024,256]{1,0:T(8,128)(2,1)}, u32[]{:S(2)}) copy-start(bf16[1024,256]{1,0:T(8,128)(2,1)} %param.13) | copy-start | bytes 1572868
  70.7 2.3 copy-start.4
  223.7 5.4 %copy-start.3 = (f32[1024,256]{1,0:T(8,128)S(1)}, f32[1024,256]{1,0:T(8,128)}, u32[]{:S(2)}) copy-start(f32[1024,256]{1,0:T(8,128)} %get-tuple-element.33) | copy-start | bytes 3145732
Sparse Core Ops, SparseCore 0:
  75.8 147.8 all-reduce.3
where the time goes:
time: 237 us
  waiting for transfers between devices  107 us (45%)
  blocking collectives  95.8 us (40%)
  between operations  16.3 us (7%)
  matrix products  8.75 us (4%)
  local copies, waits for them, and re-layouts  6.43 us (3%)
  other arithmetic  3.09 us (1%)
    psum x1, waiting for transfers between devices, shards(): lax.psum((grad_first, grad_bias, grad_second, loss_part), ('dp', 'span'))  107 us
    psum x1, blocking collectives, shards(): lax.psum((grad_first, grad_bias, grad_second, loss_part), ('dp', 'span'))  40.8 us
    all_gather x1, blocking collectives, shards(): lax.all_gather(key_rows, 'span', axis=0, tiled=True)  16.3 us
    psum x1, blocking collectives, shards(): level_counts = lax.psum(jnp.sum(onehot, axis=0), 'span')  13.5 us
    all_gather x1, blocking collectives, shards(): lax.all_gather(in_list, 'span', axis=0, tiled=True)  9.58 us
    all_gather x1, blocking collectives, shards(): lax.all_gather(row_weight, 'span', axis=0, tiled=True)  7.98 us
    all_gather x1, blocking collectives, shards(): lax.all_gather(mask_half, 'span', axis=0, tiled=True)  7.71 us
    unnamed x15, local copies, waits for them, and re-layouts  6.43 us
  transfers between devices with their start and end apart: 1, of which 1 were waited for; matrix products, arithmetic and copies ran while one was open for 0% of the time, Pallas kernels for 0%

commit v1 on v0

--- a/solution.py
+++ b/solution.py
@@ -3,10 +3,247 @@
 import jax
 import jax.numpy as jnp
 from jax import lax
+from jax.experimental import pallas as pl
+from jax.experimental.pallas import tpu as pltpu
 from jax.sharding import PartitionSpec as P
 
 gain_values = (0.0, 1.0, 3.0, 7.0, 15.0)
 log_two = math.log(2.0)
+
+
+def greet_peers(place, chips, spans):
+    core, chip, span = place
+    barrier = pltpu.get_barrier_semaphore()
+    peers = [{"dp": 2 * chip + 1 - core, "span": span}]
+    peers += [{"dp": 2 * lax.rem(chip + k, chips) + core, "span": span} for k in range(1, chips)]
+    peers += [{"dp": 2 * chip + core, "span": lax.rem(span + k, spans)} for k in range(1, spans)]
+    for peer in peers:
+        pl.semaphore_signal(barrier, inc=1, device_id=peer, device_id_type=pl.DeviceIdType.MESH)
+    pl.semaphore_wait(barrier, len(peers))
+
+
+def rows_at(start, size):
+    return pl.ds(pl.multiple_of(start, size), size)
+
+
+def owners_of(rows, chips, spans):
+    block = rows // 2 // chips
+    return min(spans, block // 16)
+
+
+class Reducer:
+    def __init__(self, place, chips, spans, read, result, small, small_out, scratch):
+        self.core, self.chip, self.span = place
+        self.chips, self.spans = chips, spans
+        self.read, self.result = read, result
+        self.small, self.small_out = small, small_out
+        (
+            self.pair_buf, self.pair_in, self.half_sum, self.half_buf, self.chip_in,
+            self.block_sum, self.block_buf, self.span_in,
+            self.small_pair, self.small_chip, self.small_span,
+            self.pair_s, self.pair_r, self.chip_s, self.chip_r, self.span_s, self.span_r,
+            self.small_s, self.small_r,
+        ) = scratch
+        self.half = self.pair_buf.shape[1]
+        self.block = self.half // chips
+        self.part = self.span_in.shape[2]
+        self.owners = self.block // self.part
+        self.copies = {}
+
+    def copy(self, key, src, dst, send, recv, dp=None, span=None):
+        peer = {
+            "dp": 2 * self.chip + self.core if dp is None else dp,
+            "span": self.span if span is None else span,
+        }
+        made = pltpu.make_async_remote_copy(
+            src_ref=src, dst_ref=dst, send_sem=send, recv_sem=recv,
+            device_id=peer, device_id_type=pl.DeviceIdType.MESH,
+        )
+        made.start()
+        self.copies.setdefault(key, []).append(made)
+
+    def settle(self, key):
+        for made in self.copies.pop(key, []):
+            made.wait()
+
+    def partner(self):
+        return 2 * self.chip + 1 - self.core
+
+    def other_chip(self, k):
+        return 2 * lax.rem(self.chip + k, self.chips) + self.core
+
+    def pair_out(self, p):
+        self.pair_buf[p] = self.read(p, rows_at((1 - self.core) * self.half, self.half)).astype(jnp.bfloat16)
+        self.copy(("pair", p), self.pair_buf.at[p], self.pair_in.at[p], self.pair_s.at[0, p], self.pair_r.at[0, p], dp=self.partner())
+
+    def chip_out(self, p):
+        self.settle(("pair", p))
+        own = self.read(p, rows_at(self.core * self.half, self.half))
+        total = own + self.pair_in[p].astype(jnp.float32)
+        self.half_sum[p] = total
+        self.half_buf[p] = total.astype(jnp.bfloat16)
+        for k in range(1, self.chips):
+            rows = rows_at(lax.rem(self.chip + k, self.chips) * self.block, self.block)
+            self.copy(("chip", p), self.half_buf.at[p, rows], self.chip_in.at[p, k - 1], self.chip_s.at[0, p, k - 1], self.chip_r.at[0, p, k - 1], dp=self.other_chip(k))
+
+    def span_out(self, p):
+        self.settle(("chip", p))
+        total = self.half_sum[p, rows_at(self.chip * self.block, self.block)]
+        for k in range(1, self.chips):
+            total = total + self.chip_in[p, k - 1].astype(jnp.float32)
+        self.block_sum[p] = total
+        self.block_buf[p] = total.astype(jnp.bfloat16)
+        for k in range(1, self.spans):
+            to = lax.rem(self.span + k, self.spans)
+            rows = rows_at(lax.rem(to, self.owners) * self.part, self.part)
+            self.copy(("span", p), self.block_buf.at[p, rows], self.span_in.at[p, k - 1], self.span_s.at[0, p, k - 1], self.span_r.at[0, p, k - 1], span=to)
+
+    def span_back(self, p):
+        self.settle(("span", p))
+        mine = lax.rem(self.span, self.owners)
+        rows = rows_at(mine * self.part, self.part)
+        if self.owners == self.spans:
+            total = self.block_sum[p, rows]
+        else:
+            total = self.block_buf[p, rows].astype(jnp.float32)
+        for k in range(1, self.spans):
+            total = total + self.span_in[p, k - 1].astype(jnp.float32)
+        start = self.core * self.half + self.chip * self.block + mine * self.part
+        place = self.result(p, rows_at(start, self.part))
+        place[...] = total.astype(jnp.bfloat16)
+        for k in range(1, self.owners):
+            to = self.span - mine + lax.rem(mine + k, self.owners)
+            self.copy(("span_back", p), place, place, self.span_s.at[1, p, k - 1], self.span_r.at[1, p, k - 1], span=to)
+
+    def chip_back(self, p):
+        self.settle(("span_back", p))
+        place = self.result(p, rows_at(self.core * self.half + self.chip * self.block, self.block))
+        for k in range(1, self.chips):
+            self.copy(("chip_back", p), place, place, self.chip_s.at[1, p, k - 1], self.chip_r.at[1, p, k - 1], dp=self.other_chip(k))
+
+    def pair_back(self, p):
+        self.settle(("chip_back", p))
+        place = self.result(p, rows_at(self.core * self.half, self.half))
+        self.copy(("pair_back", p), place, place, self.pair_s.at[1, p], self.pair_r.at[1, p], dp=self.partner())
+
+    def small_first(self):
+        self.small_pair[self.core] = self.small()
+        place = self.small_pair.at[self.core]
+        self.copy("small0", place, place, self.small_s.at[0], self.small_r.at[0], dp=self.partner())
+
+    def small_second(self):
+        self.settle("small0")
+        self.small_chip[self.chip] = self.small_pair[0] + self.small_pair[1]
+        place = self.small_chip.at[self.chip]
+        for k in range(1, self.chips):
+            self.copy("small1", place, place, self.small_s.at[k], self.small_r.at[k], dp=self.other_chip(k))
+
+    def small_third(self):
+        self.settle("small1")
+        total = self.small_chip[0]
+        for k in range(1, self.chips):
+            total = total + self.small_chip[k]
+        self.small_span[self.span] = total
+        place = self.small_span.at[self.span]
+        for k in range(1, self.spans):
+            at = self.chips + k - 1
+            self.copy("small2", place, place, self.small_s.at[at], self.small_r.at[at], span=lax.rem(self.span + k, self.spans))
+
+    def small_last(self):
+        self.settle("small2")
+        total = self.small_span[0]
+        for k in range(1, self.spans):
+            total = total + self.small_span[k]
+        self.small_out[...] = total
+
+
+def reducer_scratch(pieces, rows, width, chips, spans, small_shape):
+    half = rows // 2
+    block = half // chips
+    part = block // owners_of(rows, chips, spans)
+    vmem, dma = pltpu.VMEM, pltpu.SemaphoreType.DMA
+    return [
+        vmem((pieces, half, width), jnp.bfloat16),
+        vmem((pieces, half, width), jnp.bfloat16),
+        vmem((pieces, half, width), jnp.float32),
+        vmem((pieces, half, width), jnp.bfloat16),
+        vmem((pieces, chips - 1, block, width), jnp.bfloat16),
+        vmem((pieces, block, width), jnp.float32),
+        vmem((pieces, block, width), jnp.bfloat16),
+        vmem((pieces, spans - 1, part, width), jnp.bfloat16),
+        vmem((2,) + small_shape, jnp.float32),
+        vmem((chips,) + small_shape, jnp.float32),
+        vmem((spans,) + small_shape, jnp.float32),
+        dma((2, pieces)), dma((2, pieces)),
+        dma((2, pieces, chips - 1)), dma((2, pieces, chips - 1)),
+        dma((2, pieces, spans - 1)), dma((2, pieces, spans - 1)),
+        dma((chips + spans,)), dma((chips + spans,)),
+    ]
+
+
+def finish_reduce(red, pieces):
+    red.small_second()
+    for p in range(pieces):
+        red.span_out(p)
+    red.small_third()
+    for p in range(pieces):
+        red.span_back(p)
+    red.small_last()
+    for p in range(pieces):
+        red.chip_back(p)
+    for p in range(pieces):
+        red.pair_back(p)
+    for p in range(pieces):
+        red.settle(("pair_back", p))
+
+
+def sum_kernel(chips, spans, first, second, small, first_out, second_out, small_out, *scratch):
+    dp = lax.axis_index("dp")
+    place = (lax.rem(dp, 2), dp // 2, lax.axis_index("span"))
+    width = second.shape[1]
+    pieces = 1 + first.shape[1] // width
+
+    def read(p, rows):
+        return second[rows, :] if p == 0 else first[rows, pl.ds((p - 1) * width, width)]
+
+    def result(p, rows):
+        return second_out.at[rows] if p == 0 else first_out.at[rows, pl.ds((p - 1) * width, width)]
+
+    red = Reducer(place, chips, spans, read, result, lambda: small[...], small_out, scratch)
+    greet_peers(place, chips, spans)
+    for p in range(pieces):
+        red.pair_out(p)
+    red.small_first()
+    for p in range(pieces):
+        red.chip_out(p)
+    finish_reduce(red, pieces)
+
+
+def sum_over_devices(first, bias, second, loss):
+    chips, spans = lax.axis_size("dp") // 2, lax.axis_size("span")
+    rows, width = second.shape
+    pieces = 1 + first.shape[1] // width
+    small = jnp.concatenate([bias.reshape(-1, 128), jnp.broadcast_to(loss, (8, 128))], axis=0)
+    in_vmem = pl.BlockSpec(memory_space=pltpu.VMEM)
+    first_sum, second_sum, small_sum = pl.pallas_call(
+        lambda *refs: sum_kernel(chips, spans, *refs),
+        name="device_sum",
+        out_shape=(
+            jax.ShapeDtypeStruct(first.shape, jnp.bfloat16),
+            jax.ShapeDtypeStruct(second.shape, jnp.bfloat16),
+            jax.ShapeDtypeStruct(small.shape, jnp.float32),
+        ),
+        in_specs=[in_vmem] * 3,
+        out_specs=(in_vmem,) * 3,
+        scratch_shapes=reducer_scratch(pieces, rows, width, chips, spans, small.shape),
+        compiler_params=pltpu.CompilerParams(collective_id=0, has_side_effects=True, vmem_limit_bytes=60 << 20),
+    )(first, second, small)
+    return (
+        first_sum.astype(jnp.float32),
+        small_sum[:-8].reshape(bias.shape),
+        second_sum.astype(jnp.float32),
+        small_sum[-8, 0],
+    )
 
 
 def level_onehot(labels):
@@ -103,8 +340,8 @@
     grad_pre = jnp.where(pre_act > 0.0, back_hidden, 0.0).astype(jnp.bfloat16)
     grad_bias = jnp.sum(grad_pre.astype(jnp.float32), axis=0)
     grad_first = jnp.einsum("cd,ch->dh", row_feats, grad_pre, preferred_element_type=jnp.float32)
-    total_first, total_bias, total_second, loss = lax.psum(
-        (grad_first, grad_bias, grad_second, loss_part), ("dp", "span")
+    total_first, total_bias, total_second, loss = sum_over_devices(
+        grad_first, grad_bias, grad_second, loss_part
     )
     return (loss, total_first, total_bias, total_second)
 

time: 237 us -> 127 us (0.54)
  waiting for transfers between devices: 107 us -> 0 us
  Pallas kernels: 0 us -> 46.7 us
  blocking collectives: 95.8 us -> 53.7 us
  between operations: 16.3 us -> 2.88 us
  other arithmetic: 3.09 us -> 9.26 us
  local copies, waits for them, and re-layouts: 6.43 us -> 3.09 us
    psum x1 -> x0, waiting for transfers between devices: 107 us -> none  [shards(): lax.psum((grad_first, grad_bias, grad_second, loss_part), ('dp', 'span'))]
    pallas_call x0 -> x1, Pallas kernels: none -> 46.7 us  [sum_over_devices(): pl.pallas_call(lambda *refs: sum_kernel(chips, spans, *refs), name='devic...]
    psum x1 -> x0, blocking collectives: 40.8 us -> none  [shards(): lax.psum((grad_first, grad_bias, grad_second, loss_part), ('dp', 'span'))]
    unnamed x15 -> x11, local copies, waits for them, and re-layouts: 6.43 us -> 0.03 us
    convert_element_type x0 -> x2, other arithmetic: none -> 6.15 us  [the longest x1 4.07 us: sum_over_devices(): first_sum.astype(jnp.float32)]
  transfers between devices with their start and end apart: 1 -> 0, of which waited for: 1 -> 0; matrix products, arithmetic and copies ran while one was open for 0% -> 0% of each run, Pallas kernels for 0% -> 0%
where the time goes in v1:
time: 127 us; the launch traced here: 126 us
  blocking collectives  53.7 us (42%)
  Pallas kernels  46.7 us (37%)
  matrix products  10 us (8%)
  other arithmetic  9.26 us (7%)
  local copies, waits for them, and re-layouts  3.09 us (2%)
  between operations  2.88 us (2%)
    pallas_call x1, Pallas kernels, sum_over_devices(): pl.pallas_call(lambda *refs: sum_kernel(chips, spans, *refs), name='devic...  46.7 us
    all_gather x1, blocking collectives, shards(): lax.all_gather(key_rows, 'span', axis=0, tiled=True)  15 us
    psum x1, blocking collectives, shards(): level_counts = lax.psum(jnp.sum(onehot, axis=0), 'span')  13.5 us
    all_gather x1, blocking collectives, shards(): lax.all_gather(in_list, 'span', axis=0, tiled=True)  9.58 us
    all_gather x1, blocking collectives, shards(): lax.all_gather(row_weight, 'span', axis=0, tiled=True)  8.13 us
    all_gather x1, blocking collectives, shards(): lax.all_gather(mask_half, 'span', axis=0, tiled=True)  7.57 us
    convert_element_type x1, other arithmetic, sum_over_devices(): first_sum.astype(jnp.float32)  4.07 us
    dot_general x1, matrix products, shards(): jnp.einsum('cd,ch->dh', row_feats, grad_pre, preferred_element_type=jnp.f...  2.77 us

profile of v1, /device:TPU:0, one launch (start us, length us, event | category | flops | bytes accessed | tf_op | source)
XLA Modules:
  0.0 125.7 jit_solution(14521825104645668623)
XLA Ops:
  0.6 0.0 copy-start
  1.5 0.9 select_reduce_fusion.1
  2.4 13.5 %psum.7 = f32[5]{0:T(128)S(1)} all-reduce(f32[5]{0:T(128)S(1)} %get-tuple-element.10), channel_id=1, replica_groups=mesh['dp'=8,'span'=4] {'span'}, use_global_device_ids=true, to_apply=%region_2.0 | all-reduce | flops 5 | bytes 40 | tf_op jit(solution)/shard_map/psum | solution.py:303
  15.8 0.1 select_reduce_fusion.2
  15.9 7.6 %all-gather = bf16[4,1,256]{2,1,0:T(2,128)(2,1)S(1)} all-gather(bf16[1,1,256]{2,1,0:T(2,128)(2,1)S(1)} %reshape.52), channel_id=1, replica_groups=mesh['dp'=8,'span'=4] {'span'}, dimensions={0}, use_global_device_ids=true | all-gather | bytes 2560 | tf_op jit(solution)/shard_map/all_gather | solution.py:313
  23.5 9.6 %all-gather.2 = f32[4,1,256]{2,1,0:T(1,128)S(1)} all-gather(f32[1,1,256]{2,1,0:T(1,128)S(1)} %bitcast.30), channel_id=1, replica_groups=mesh['dp'=8,'span'=4] {'span'}, dimensions={0}, use_global_device_ids=true | all-gather | bytes 5120 | tf_op jit(solution)/shard_map/all_gather | solution.py:326
  33.1 0.2 select_reduce_fusion
  33.3 1.3 %multiply_reduce_fusion.1 = f32[]{:T(128)} fusion(f32[5]{0:T(128)S(1)} %select_reduce_fusion, f32[5]{0:T(128)} %constant.35.clone), kind=kLoop, calls=%fused_computation.35 | loop fusion | flops 9 | bytes 44 | tf_op jit(solution)/shard_map/reduce_sum | solution.py:262
  35.2 0.0 copy-done
  35.2 0.0 copy-start.1
  35.3 1.8 %convolution_add_fusion = f32[256,1024]{1,0:T(8,128)S(1)} fusion(bf16[1024,1024]{1,0:T(8,128)(2,1)S(1)} %copy-done, bf16[1,256,1024]{2,1,0:T(8,128)(2,1)} %param.8, f32[1024]{0:T(1024)} %param.12), kind=kOutput, calls=%fused_computation.4 | convolution fusion | flops 537133056 | bytes 3674112 | tf_op jit(solution)/shard_map/dot_general | solution.py:305
  37.1 0.0 copy-done.1
  37.1 0.4 convolution_convert_fusion
  37.5 15.0 %all_gather.13 = bf16[1024,256]{0,1:T(8,128)(2,1)S(1)} all-gather(bf16[256,256]{0,1:T(8,128)(2,1)S(1)} %pad_maximum_fusion), channel_id=1, replica_groups=mesh['dp'=8,'span'=4] {'span'}, dimensions={0}, use_global_device_ids=true | all-gather | bytes 655360 | tf_op jit(solution)/shard_map/all_gather | solution.py:332
  52.5 0.0 copy-start.4
  52.5 1.4 %multiply_reduce_fusion = (f32[256]{0:T(256)S(1)}, f32[256,1024]{1,0:T(8,128)}) fusion(f32[1024]{0:T(1024)S(1)} %bitcast.33, bf16[256,256]{0,1:T(8,128)(2,1)S(1)} %convolution_convert_fusion, bf16[1024,256]{0,1:T(8,128)(2,1)S(1)} %all_gather.13), kind=kOutput, calls=%fused_computation.12 | convolution fusion | flops 135528192 | bytes 1709056 | tf_op jit(solution)/shard_map/ik,jk->ij/dot_general | solution.py:275
  53.9 0.0 copy-done.4
  53.9 0.6 fusion.10
  55.2 8.1 %all-gather.1 = f32[4,1,256]{2,1,0:T(1,128)S(1)} all-gather(f32[1,1,256]{2,1,0:T(1,128)S(1)} %bitcast.34), channel_id=1, replica_groups=mesh['dp'=8,'span'=4] {'span'}, dimensions={0}, use_global_device_ids=true | all-gather | bytes 5120 | tf_op jit(solution)/shard_map/all_gather | solution.py:325
  63.3 0.0 copy-start.2
  63.3 2.0 %fusion.1 = bf16[256,256]{1,0:T(8,128)(2,1)S(1)} fusion(bf16[1024,256]{0,1:T(8,128)(2,1)} %copy-done.4, f32[256,1024]{1,0:T(8,128)} %get-tuple-element.17, f32[1024]{0:T(1024)S(1)} %bitcast.31, f32[256]{0:T(256)S(1)} %get-tuple-element.15, f32[1024]{0:T(1024)S(1)} %bitcast.32, f32[256]{0:T(256)S(1)} %compare_convert_fusion), kind=kOutput, calls=%fused_computation.8 | convolution fusion | flops 136970240 | bytes 1714176 | tf_op jit(solution)/shard_map/dot_general | solution.py:285
  65.3 0.0 copy-done.2
  65.3 0.0 copy-start.3
  65.3 0.3 convert_reduce_fusion
  65.7 1.3 %fusion.7.refs_1_ = f32[1024,256]{1,0:T(8,128)} fusion(bf16[256,256]{1,0:T(8,128)(2,1)S(1)} %fusion.1, f32[256,1024]{1,0:T(8,128)S(1)} %convolution_add_fusion), kind=kOutput, calls=%fused_computation.16 | convolution fusion | flops 134742016 | bytes 2228224 | tf_op jit(solution)/shard_map/ch,ce->he/dot_general | solution.py:338
  67.0 0.6 concatenate.7.refs_2_
  67.6 0.0 copy-done.3
  67.6 2.8 %convolution_bitcast_fusion.refs_0_ = f32[1024,1024]{1,0:T(8,128)} fusion(bf16[256,1024]{1,0:T(8,128)(2,1)S(1)} %get-tuple-element.19, bf16[1,256,1024]{2,1,0:T(8,128)(2,1)S(1)} %copy-done.3), kind=kOutput, calls=%fused_computation | convolution fusion | flops 536870912 | bytes 5242880 | tf_op jit(solution)/shard_map/cd,ch->dh/dot_general | solution.py:342
  70.4 46.7 %device_sum.1 = (bf16[1024,1024]{1,0:T(8,128)(2,1)}, bf16[1024,256]{1,0:T(8,128)(2,1)}, f32[16,128]{1,0:T(8,128)}) custom-call(f32[1024,1024]{1,0:T(8,128)} %convolution_bitcast_fusion.refs_0_, f32[1024,256]{1,0:T(8,128)} %fusion.7.refs_1_, f32[16,128]{1,0:T(8,128)} %concatenate.7.refs_2_), custom_call_target="tpu_custom_call" | custom-call | tf_op jit(solution)/shard_map/device_sum/pallas_call | solution.py:228
  117.1 1.2 slice.14
  118.2 1.3 %slice_bitcast_fusion = f32[1024]{0:T(1024)} fusion(f32[16,128]{1,0:T(8,128)} %get-tuple-element.7), kind=kLoop, calls=%fused_computation.24 | loop fusion | bytes 8192 | tf_op jit(solution)/shard_map/reshape | solution.py:243
  119.5 2.1 %convert_element_type.64 = f32[1024,256]{1,0:T(8,128)} convert(bf16[1024,256]{1,0:T(8,128)(2,1)} %get-tuple-element.9) | non-fusion elementwise | flops 262144 | bytes 1572864 | tf_op jit(solution)/shard_map/convert_element_type | solution.py:244
  121.6 4.1 %convert_element_type.63 = f32[1024,1024]{1,0:T(8,128)} convert(bf16[1024,1024]{1,0:T(8,128)(2,1)} %get-tuple-element.8) | non-fusion elementwise | flops 1048576 | bytes 6291456 | tf_op jit(solution)/shard_map/convert_element_type | solution.py:242
  (9 shorter events, 0.1 us)
Async XLA Ops:
  0.6 34.6 %copy-start = (bf16[1024,1024]{1,0:T(8,128)(2,1)S(1)}, bf16[1024,1024]{1,0:T(8,128)(2,1)}, u32[]{:S(2)}) copy-start(bf16[1024,1024]{1,0:T(8,128)(2,1)} %param.11) | copy-start | bytes 6291460
  35.2 1.8 %copy-start.1 = (bf16[1024,256]{1,0:T(8,128)(2,1)S(1)}, bf16[1024,256]{1,0:T(8,128)(2,1)}, u32[]{:S(2)}) copy-start(bf16[1024,256]{1,0:T(8,128)(2,1)} %param.13) | copy-start | bytes 1572868
  52.5 1.4 %copy-start.4 = (bf16[1024,256]{0,1:T(8,128)(2,1)}, bf16[1024,256]{0,1:T(8,128)(2,1)S(1)}, u32[]{:S(2)}) copy-start(bf16[1024,256]{0,1:T(8,128)(2,1)S(1)} %all_gather.13) | copy-start | bytes 1572868
  63.3 2.0 %copy-start.2 = (bf16[1024,256]{1,0:T(8,128)(2,1)S(1)}, bf16[1024,256]{1,0:T(8,128)(2,1)}, u32[]{:S(2)}) copy-start(bf16[1024,256]{1,0:T(8,128)(2,1)} %param.13) | copy-start | bytes 1572868
  65.3 2.3 %copy-start.3 = (bf16[1,256,1024]{2,1,0:T(8,128)(2,1)S(1)}, bf16[1,256,1024]{2,1,0:T(8,128)(2,1)}, u32[]{:S(2)}) copy-start(bf16[1,256,1024]{2,1,0:T(8,128)(2,1)} %param.8) | copy-start | bytes 1572868

commit v2 on v1

--- a/solution.py
+++ b/solution.py
@@ -19,7 +19,7 @@
     peers += [{"dp": 2 * chip + core, "span": lax.rem(span + k, spans)} for k in range(1, spans)]
     for peer in peers:
         pl.semaphore_signal(barrier, inc=1, device_id=peer, device_id_type=pl.DeviceIdType.MESH)
-    pl.semaphore_wait(barrier, len(peers))
+    return lambda: pl.semaphore_wait(barrier, len(peers))
 
 
 def rows_at(start, size):
@@ -197,153 +197,195 @@
         red.settle(("pair_back", p))
 
 
-def sum_kernel(chips, spans, first, second, small, first_out, second_out, small_out, *scratch):
-    dp = lax.axis_index("dp")
-    place = (lax.rem(dp, 2), dp // 2, lax.axis_index("span"))
-    width = second.shape[1]
-    pieces = 1 + first.shape[1] // width
-
-    def read(p, rows):
-        return second[rows, :] if p == 0 else first[rows, pl.ds((p - 1) * width, width)]
-
-    def result(p, rows):
-        return second_out.at[rows] if p == 0 else first_out.at[rows, pl.ds((p - 1) * width, width)]
+def dot(lhs, rhs, dims):
+    return lax.dot_general(lhs, rhs, (dims, ((), ())), preferred_element_type=jnp.float32)
+
+
+def ideal_gain(counts, list_len):
+    places = (1 + lax.broadcasted_iota(jnp.int32, (1, list_len), 1)).astype(jnp.float32)
+    discount = log_two / jnp.log(1.0 + places)
+    total = jnp.zeros((1, 1), jnp.float32)
+    start = jnp.zeros((1, 1), jnp.float32)
+    for level in reversed(range(len(gain_values))):
+        finish = start + counts[level : level + 1, 0:1]
+        inside = (places > start) & (places <= finish)
+        total = total + gain_values[level] * jnp.sum(jnp.where(inside, discount, 0.0), axis=1, keepdims=True)
+        start = finish
+    return jnp.maximum(total, 1.0)
+
+
+def step_kernel(
+    chips, spans, lengths, labels, features_hbm, w_first_hbm, b_first, w_second_hbm,
+    first_out, second_out, small_out,
+    feats, w_first, w_second, feats_t, hidden_t, pre, hidden, emb, keys, slopes, weights, counts, grads, small,
+    load_sem, key_s, key_r, weight_s, weight_r, count_s, count_r, *scratch,
+):
+    dp, span = lax.axis_index("dp"), lax.axis_index("span")
+    place = (lax.rem(dp, 2), dp // 2, span)
+    rows = feats.shape[0]
+    width = w_second.shape[1]
+    hid = w_first.shape[1]
+    half_width = width // 2
+    pair_scale = 1.0 / math.sqrt(half_width)
+    pieces = 1 + hid // width
+    list_count, list_len = 2 * chips, rows * spans
+    loads = [
+        pltpu.make_async_copy(src, dst, load_sem.at[n])
+        for n, (src, dst) in enumerate(
+            ((features_hbm.at[0], feats), (w_first_hbm, w_first), (w_second_hbm, w_second))
+        )
+    ]
+    for load in loads:
+        load.start()
+    enter = greet_peers(place, chips, spans)
+
+    def to_peers(make_src, dst, send, recv):
+        made = []
+        for k in range(1, spans):
+            copy = pltpu.make_async_remote_copy(
+                src_ref=make_src, dst_ref=dst.at[k], send_sem=send.at[k - 1], recv_sem=recv.at[k - 1],
+                device_id={"dp": dp, "span": lax.rem(span + k, spans)}, device_id_type=pl.DeviceIdType.MESH,
+            )
+            copy.start()
+            made.append(copy)
+        return made
+
+    length = lengths[0]
+    slots = lax.broadcasted_iota(jnp.int32, (1, rows), 1)
+
+    def live_row(k):
+        owner = lax.rem(span - k + spans, spans)
+        return (owner * rows + slots < length).astype(jnp.float32)
+
+    own_live = live_row(0)
+    live_col = (span * rows + lax.broadcasted_iota(jnp.int32, (rows, 1), 0) < length).astype(jnp.float32)
+    eye = lax.broadcasted_iota(jnp.int32, (rows, rows), 0) == lax.broadcasted_iota(jnp.int32, (rows, rows), 1)
+    label_row = labels[...].astype(jnp.float32)
+    label_col = jnp.sum(jnp.where(eye, label_row, 0.0), axis=1, keepdims=True)
+    gain = jnp.zeros((rows, 1), jnp.float32)
+    for level, value in enumerate(gain_values):
+        gain = gain + jnp.where(label_col == level, value, 0.0)
+    gain = gain * live_col
+    levels = lax.broadcasted_iota(jnp.int32, (8, rows), 0).astype(jnp.float32)
+    level_counts = jnp.sum(jnp.where(levels == label_row, own_live, 0.0), axis=1, keepdims=True)
+    counts[0] = jnp.broadcast_to(level_counts, counts.shape[1:])
+
+    loads[0].wait()
+    loads[1].wait()
+    for p in range(pieces - 1):
+        cols = pl.ds(p * width, width)
+        pre_act = dot(feats[...], w_first[:, cols], ((1,), (0,))) + b_first[:, cols]
+        pre[:, cols] = pre_act
+        hidden[:, cols] = jnp.maximum(pre_act, 0.0).astype(jnp.bfloat16)
+    loads[2].wait()
+    row_emb = dot(hidden[...], w_second[...], ((1,), (0,))).astype(jnp.bfloat16)
+    emb[...] = row_emb
+    keys[0] = jnp.concatenate([row_emb[:, half_width:], -row_emb[:, :half_width]], axis=1)
+    enter()
+    key_copies = to_peers(keys.at[0], keys, key_s, key_r)
+    count_copies = to_peers(counts.at[0], counts, count_s, count_r)
+    feats_t[...] = feats[...].T
+    hidden_t[...] = hidden[...].T
+
+    rank = jnp.full((rows, 1), 0.5, jnp.float32)
+    for k in range(spans):
+        if k:
+            key_copies[k - 1].wait()
+        logits = dot(emb[...], keys[k], ((1,), (1,))) * pair_scale
+        below = jax.nn.sigmoid(-logits)
+        slopes[k] = below * (1.0 - below)
+        rank = rank + jnp.sum(below * live_row(k), axis=1, keepdims=True)
+    for copy in count_copies:
+        copy.wait()
+    all_counts = counts[0]
+    for k in range(1, spans):
+        all_counts = all_counts + counts[k]
+    ideal = ideal_gain(all_counts, list_len)
+    log_rank = jnp.log(1.0 + rank)
+    weight = gain / (ideal * list_count) * log_two / ((1.0 + rank) * log_rank * log_rank)
+    weights[0] = jnp.broadcast_to(jnp.sum(jnp.where(eye, weight, 0.0), axis=0, keepdims=True), weights.shape[1:])
+    weight_copies = to_peers(weights.at[0], weights, weight_s, weight_r)
+    dcg = jnp.sum(gain * log_two / log_rank, axis=0, keepdims=True)
+    loss_part = (1.0 / spans - dcg / ideal) / list_count
+    small[:, pl.ds(hid, 128)] = jnp.broadcast_to(loss_part, (1, 128))
+
+    total = jnp.zeros((rows, width), jnp.float32)
+    for k in range(spans):
+        if k:
+            weight_copies[k - 1].wait()
+        pair_grad = slopes[k] * (live_col * weights[k, 0:1, :] - weight * live_row(k))
+        total = total + dot(pair_grad.astype(jnp.bfloat16), keys[k], ((1,), (0,)))
+    grad_emb = (total * pair_scale).astype(jnp.bfloat16)
+
+    def read(p, at):
+        return grads[p, at, :]
+
+    def result(p, at):
+        return second_out.at[at] if p == 0 else first_out.at[at, pl.ds((p - 1) * width, width)]
 
     red = Reducer(place, chips, spans, read, result, lambda: small[...], small_out, scratch)
-    greet_peers(place, chips, spans)
-    for p in range(pieces):
+    grads[0] = dot(hidden_t[...], grad_emb, ((1,), (0,)))
+    red.pair_out(0)
+    for p in range(1, pieces):
+        cols = pl.ds((p - 1) * width, width)
+        back = dot(grad_emb, w_second[cols, :], ((1,), (1,)))
+        grad_pre = jnp.where(pre[:, cols] > 0.0, back, 0.0).astype(jnp.bfloat16)
+        small[:, cols] = jnp.sum(grad_pre.astype(jnp.float32), axis=0, keepdims=True)
+        grads[p] = dot(feats_t[...], grad_pre, ((1,), (0,)))
         red.pair_out(p)
+        red.chip_out(p - 1)
     red.small_first()
-    for p in range(pieces):
-        red.chip_out(p)
+    red.chip_out(pieces - 1)
     finish_reduce(red, pieces)
 
 
-def sum_over_devices(first, bias, second, loss):
+def shards(features, lengths, labels, w_first, b_first, w_second):
     chips, spans = lax.axis_size("dp") // 2, lax.axis_size("span")
-    rows, width = second.shape
-    pieces = 1 + first.shape[1] // width
-    small = jnp.concatenate([bias.reshape(-1, 128), jnp.broadcast_to(loss, (8, 128))], axis=0)
+    rows, depth = features.shape[1:]
+    hid, width = w_second.shape
+    pieces = 1 + hid // width
+    small_shape = (1, hid + 128)
+    vmem, dma = pltpu.VMEM, pltpu.SemaphoreType.DMA
     in_vmem = pl.BlockSpec(memory_space=pltpu.VMEM)
+    in_place = pl.BlockSpec(memory_space=pl.ANY)
     first_sum, second_sum, small_sum = pl.pallas_call(
-        lambda *refs: sum_kernel(chips, spans, *refs),
-        name="device_sum",
+        lambda *refs: step_kernel(chips, spans, *refs),
+        name="rank_step",
         out_shape=(
-            jax.ShapeDtypeStruct(first.shape, jnp.bfloat16),
-            jax.ShapeDtypeStruct(second.shape, jnp.bfloat16),
-            jax.ShapeDtypeStruct(small.shape, jnp.float32),
+            jax.ShapeDtypeStruct((depth, hid), jnp.bfloat16),
+            jax.ShapeDtypeStruct((hid, width), jnp.bfloat16),
+            jax.ShapeDtypeStruct(small_shape, jnp.float32),
         ),
-        in_specs=[in_vmem] * 3,
+        in_specs=[pl.BlockSpec(memory_space=pltpu.SMEM), in_vmem, in_place, in_place, in_vmem, in_place],
         out_specs=(in_vmem,) * 3,
-        scratch_shapes=reducer_scratch(pieces, rows, width, chips, spans, small.shape),
+        scratch_shapes=[
+            vmem((rows, depth), jnp.bfloat16),
+            vmem((depth, hid), jnp.bfloat16),
+            vmem((hid, width), jnp.bfloat16),
+            vmem((depth, rows), jnp.bfloat16),
+            vmem((hid, rows), jnp.bfloat16),
+            vmem((rows, hid), jnp.float32),
+            vmem((rows, hid), jnp.bfloat16),
+            vmem((rows, width), jnp.bfloat16),
+            vmem((spans, rows, width), jnp.bfloat16),
+            vmem((spans, rows, rows), jnp.float32),
+            vmem((spans, 8, rows), jnp.float32),
+            vmem((spans, 8, 128), jnp.float32),
+            vmem((pieces, hid, width), jnp.float32),
+            vmem(small_shape, jnp.float32),
+            dma((3,)),
+            dma((spans - 1,)), dma((spans - 1,)), dma((spans - 1,)),
+            dma((spans - 1,)), dma((spans - 1,)), dma((spans - 1,)),
+        ]
+        + reducer_scratch(pieces, hid, width, chips, spans, small_shape),
         compiler_params=pltpu.CompilerParams(collective_id=0, has_side_effects=True, vmem_limit_bytes=60 << 20),
-    )(first, second, small)
+    )(lengths, labels, features, w_first, b_first.reshape(1, -1), w_second)
     return (
+        small_sum[0, hid],
         first_sum.astype(jnp.float32),
-        small_sum[:-8].reshape(bias.shape),
+        small_sum[0, :hid],
         second_sum.astype(jnp.float32),
-        small_sum[-8, 0],
     )
-
-
-def level_onehot(labels):
-    return (labels[..., None] == jnp.arange(5, dtype=jnp.int32)).astype(jnp.float32)
-
-
-def ideal_gain(level_counts, list_len):
-    levels = jnp.arange(5, dtype=jnp.int32)
-    above_mask = (levels[:, None] > levels[None, :]).astype(jnp.float32)
-    starts = jnp.sum(level_counts[:, None] * above_mask, axis=0)
-    finish = starts + level_counts
-    places = jnp.arange(1, list_len + 1, dtype=jnp.int32).astype(jnp.float32)
-    discount = log_two / jnp.log1p(places)
-    inside = (places[None, :] > starts[:, None]) & (places[None, :] <= finish[:, None])
-    per_level = jnp.sum(jnp.where(inside, discount[None, :], 0.0), axis=1)
-    return jnp.maximum(jnp.sum(per_level * jnp.asarray(gain_values, jnp.float32)), 1.0)
-
-
-def rank_part(row_emb, block_keys, block_mask, pair_scale):
-    logits = (
-        jnp.einsum("ik,jk->ij", row_emb, block_keys, preferred_element_type=jnp.float32)
-        * pair_scale
-    )
-    return jnp.sum(jax.nn.sigmoid(-logits) * block_mask.astype(jnp.float32)[None, :], axis=1)
-
-
-def grad_part(row_emb, row_weight, row_mask, block_keys, key_weight, key_mask, pair_scale):
-    logits = (
-        jnp.einsum("ik,jk->ij", row_emb, block_keys, preferred_element_type=jnp.float32)
-        * pair_scale
-    )
-    probab = jax.nn.sigmoid(logits)
-    pair_grad = (
-        probab
-        * (1.0 - probab)
-        * (row_mask[:, None] * key_weight[None, :] - row_weight[:, None] * key_mask[None, :])
-    )
-    return (
-        jnp.dot(pair_grad.astype(jnp.bfloat16), block_keys, preferred_element_type=jnp.float32)
-        * pair_scale
-    )
-
-
-def shards(features, lengths, labels, w_first, b_first, w_second):
-    row_feats = features[0]
-    row_count = row_feats.shape[0]
-    half_width = w_second.shape[1] // 2
-    pair_scale = 1.0 / math.sqrt(half_width)
-    span_count = lax.axis_size("span")
-    list_count = lax.axis_size("dp")
-    list_len = row_count * span_count
-    row_start = lax.axis_index("span") * row_count
-    length = lengths[0]
-    in_list = (row_start + jnp.arange(row_count, dtype=jnp.int32) < length).astype(jnp.float32)
-    onehot = level_onehot(labels[0]) * in_list[:, None]
-    gain_row = jnp.sum(onehot * jnp.asarray(gain_values, jnp.float32)[None, :], axis=1)
-    level_counts = lax.psum(jnp.sum(onehot, axis=0), "span")
-    ideal = ideal_gain(level_counts, list_len)
-    pre_act = jnp.dot(row_feats, w_first, preferred_element_type=jnp.float32) + b_first[None, :]
-    hidden = jnp.maximum(pre_act, 0.0).astype(jnp.bfloat16)
-    row_emb = jnp.dot(hidden, w_second, preferred_element_type=jnp.float32).astype(jnp.bfloat16)
-    key_rows = jnp.concatenate([row_emb[:, half_width:], -row_emb[:, :half_width]], axis=1)
-    mask_half = in_list.astype(jnp.bfloat16)
-    result = rank_part(
-        row_emb,
-        lax.all_gather(key_rows, "span", axis=0, tiled=True),
-        lax.all_gather(mask_half, "span", axis=0, tiled=True),
-        pair_scale,
-    )
-    rank_sum = result
-    soft_rank = 0.5 + rank_sum
-    log_rank = jnp.log1p(soft_rank)
-    approx_dcg = jnp.sum(gain_row * log_two / log_rank)
-    loss_part = (1.0 / span_count - approx_dcg / ideal) / list_count
-    row_weight = (
-        gain_row / (ideal * list_count) * log_two / ((1.0 + soft_rank) * log_rank * log_rank)
-    )
-    all_weight, all_live = (
-        lax.all_gather(row_weight, "span", axis=0, tiled=True),
-        lax.all_gather(in_list, "span", axis=0, tiled=True),
-    )
-    result = grad_part(
-        row_emb,
-        row_weight,
-        in_list,
-        lax.all_gather(key_rows, "span", axis=0, tiled=True),
-        all_weight,
-        all_live,
-        pair_scale,
-    )
-    grad_emb = result.astype(jnp.bfloat16)
-    grad_second = jnp.einsum("ch,ce->he", hidden, grad_emb, preferred_element_type=jnp.float32)
-    back_hidden = jnp.einsum("ce,he->ch", grad_emb, w_second, preferred_element_type=jnp.float32)
-    grad_pre = jnp.where(pre_act > 0.0, back_hidden, 0.0).astype(jnp.bfloat16)
-    grad_bias = jnp.sum(grad_pre.astype(jnp.float32), axis=0)
-    grad_first = jnp.einsum("cd,ch->dh", row_feats, grad_pre, preferred_element_type=jnp.float32)
-    total_first, total_bias, total_second, loss = sum_over_devices(
-        grad_first, grad_bias, grad_second, loss_part
-    )
-    return (loss, total_first, total_bias, total_second)
 
 
 def solution(mesh):

time: 127 us -> 75.9 us (0.60)
  blocking collectives: 53.7 us -> 0 us
  Pallas kernels: 46.7 us -> 66.7 us
  matrix products: 10 us -> 0 us
  other arithmetic: 9.26 us -> 5.17 us
  between operations: 2.88 us -> 1.29 us
    all_gather x4 -> x0, blocking collectives: 40.2 us -> none  [the longest x1 15 us: shards(): lax.all_gather(key_rows, 'span', axis=0, tiled=True)]
    pallas_call x1, Pallas kernels: 46.7 us -> 66.7 us  [shards(): pl.pallas_call(lambda *refs: step_kernel(chips, spans, *refs), name='rank...]
    psum x1 -> x0, blocking collectives: 13.5 us -> none  [shards(): level_counts = lax.psum(jnp.sum(onehot, axis=0), 'span')]
    dot_general x7 -> x0, matrix products: 10 us -> none  [the longest x1 2.77 us: shards(): jnp.einsum('cd,ch->dh', row_feats, grad_pre, preferred_element_type=jnp.f...]
    reduce_sum x5 -> x0, other arithmetic: 3.04 us -> none  [the longest x1 1.27 us: ideal_gain(): jnp.sum(per_level * jnp.asarray(gain_values, jnp.float32))]
    reshape x1 -> x0, local copies, waits for them, and re-layouts: 1.27 us -> none  [sum_over_devices(): small_sum[:-8].reshape(bias.shape)]
    convert_element_type x6 -> x2, other arithmetic: 6.18 us -> 5.17 us  [the longest x1 4.13 us: shards(): first_sum.astype(jnp.float32)]
where the time goes in v2:
time: 75.9 us; the launch traced here: 75.7 us
  Pallas kernels  66.7 us (88%)
  other arithmetic  5.17 us (7%)
  local copies, waits for them, and re-layouts  2.45 us (3%)
  between operations  1.29 us (2%)
    pallas_call x1, Pallas kernels, shards(): pl.pallas_call(lambda *refs: step_kernel(chips, spans, *refs), name='rank...  66.7 us
    convert_element_type x1, other arithmetic, shards(): first_sum.astype(jnp.float32)  4.13 us

profile of v2, /device:TPU:0, one launch (start us, length us, event | category | flops | bytes accessed | tf_op | source)
XLA Modules:
  0.0 75.7 jit_solution(932224135095198645)
XLA Ops:
  1.3 66.7 %rank_step.1 = (bf16[1024,1024]{1,0:T(8,128)(2,1)}, bf16[1024,256]{1,0:T(8,128)(2,1)}, f32[1,1152]{1,0:T(1,128)}) custom-call(s32[1]{0:T(128)S(6)} %copy.10.refs_0_, s32[1,256]{1,0:T(1,128)} %refs_1_.1, bf16[1,256,1024]{2,1,0:T(8,128)(2,1)} %refs_2_.1, bf16[1024,1024]{1,0:T(8,128)(2,1)} %refs_3_.1, f32[1,1024]{1,0:T(1,128)} %bitcast.3, bf16[1024,256]{1,0:T(8,128)(2,1)} %refs_5_.1), custom_call_target="tpu_custom_call" | custom-call | tf_op jit(solution)/shard_map/rank_step/pallas_call | solution.py:351
  68.0 1.3 %slice.7 = f32[1,1024]{1,0:T(1,128)} slice(f32[1,1152]{1,0:T(1,128)} %get-tuple-element.7), slice={[0:1], [0:1024]} | slice | bytes 8192 | tf_op jit(solution)/shard_map/slice | solution.py:386
  69.3 1.2 %slice.6 = f32[1,1]{1,0:T(1,128)} slice(f32[1,1152]{1,0:T(1,128)} %get-tuple-element.7), slice={[0:1], [1024:1025]} | slice | bytes 8 | tf_op jit(solution)/shard_map/slice | solution.py:384
  70.5 0.0 copy-start
  70.5 4.1 %convert_element_type.6 = f32[1024,1024]{1,0:T(8,128)} convert(bf16[1024,1024]{1,0:T(8,128)(2,1)} %get-tuple-element.8) | non-fusion elementwise | flops 1048576 | bytes 6291456 | tf_op jit(solution)/shard_map/convert_element_type | solution.py:385
  74.6 0.0 copy-done
  74.6 1.0 %convert_element_type.7 = f32[1024,256]{1,0:T(8,128)} convert(bf16[1024,256]{1,0:T(8,128)(2,1)S(1)} %copy-done) | non-fusion elementwise | flops 262144 | bytes 1572864 | tf_op jit(solution)/shard_map/convert_element_type | solution.py:387
Async XLA Ops:
  70.5 4.1 %copy-start = (bf16[1024,256]{1,0:T(8,128)(2,1)S(1)}, bf16[1024,256]{1,0:T(8,128)(2,1)}, u32[]{:S(2)}) copy-start(bf16[1024,256]{1,0:T(8,128)(2,1)} %get-tuple-element.9) | copy-start | bytes 1572868

commit v3 on v2

--- a/solution.py
+++ b/solution.py
@@ -182,19 +182,32 @@
 
 
 def finish_reduce(red, pieces):
-    red.small_second()
-    for p in range(pieces):
-        red.span_out(p)
-    red.small_third()
-    for p in range(pieces):
-        red.span_back(p)
-    red.small_last()
-    for p in range(pieces):
-        red.chip_back(p)
-    for p in range(pieces):
-        red.pair_back(p)
-    for p in range(pieces):
-        red.settle(("pair_back", p))
+    stages = (red.span_out, red.span_back, red.chip_back, red.pair_back, lambda p: red.settle(("pair_back", p)))
+    smalls = {0: red.small_second, 1: red.small_third, 3: red.small_last}
+    for turn in range(pieces + len(stages) - 1):
+        for lag, stage in enumerate(stages):
+            if 0 <= turn - lag < pieces:
+                stage(turn - lag)
+        if turn in smalls:
+            smalls[turn]()
+
+
+def write_kernel(first, second, small, first_out, second_out, bias_out, loss_out, first_buf, second_buf, sem):
+    parts = first_buf.shape[0]
+    rows = first_buf.shape[1]
+    copies = [pltpu.make_async_copy(second_buf, second_out, sem.at[parts])]
+    second_buf[...] = second[...].astype(jnp.float32)
+    copies[0].start()
+    for n in range(parts):
+        at = pl.ds(n * rows, rows)
+        first_buf[n] = first[at, :].astype(jnp.float32)
+        copies.append(pltpu.make_async_copy(first_buf.at[n], first_out.at[at], sem.at[n]))
+        copies[-1].start()
+    hid = bias_out.shape[1]
+    bias_out[...] = small[:, pl.ds(0, hid)]
+    loss_out[...] = small[:, pl.ds(hid, 1)]
+    for copy in copies:
+        copy.wait()
 
 
 def dot(lhs, rhs, dims):
@@ -380,12 +393,25 @@
         + reducer_scratch(pieces, hid, width, chips, spans, small_shape),
         compiler_params=pltpu.CompilerParams(collective_id=0, has_side_effects=True, vmem_limit_bytes=60 << 20),
     )(lengths, labels, features, w_first, b_first.reshape(1, -1), w_second)
-    return (
-        small_sum[0, hid],
-        first_sum.astype(jnp.float32),
-        small_sum[0, :hid],
-        second_sum.astype(jnp.float32),
-    )
+    parts = 4
+    first, second, bias, loss = pl.pallas_call(
+        write_kernel,
+        name="write_out",
+        out_shape=(
+            jax.ShapeDtypeStruct((depth, hid), jnp.float32),
+            jax.ShapeDtypeStruct((hid, width), jnp.float32),
+            jax.ShapeDtypeStruct((1, hid), jnp.float32),
+            jax.ShapeDtypeStruct((1, 1), jnp.float32),
+        ),
+        in_specs=[in_vmem] * 3,
+        out_specs=(in_place, in_place, in_vmem, in_vmem),
+        scratch_shapes=[
+            vmem((parts, depth // parts, hid), jnp.float32),
+            vmem((hid, width), jnp.float32),
+            dma((parts + 1,)),
+        ],
+    )(first_sum, second_sum, small_sum)
+    return loss[0, 0], first, bias[0], second
 
 
 def solution(mesh):

time: 75.9 us -> 73 us (0.962)
  other arithmetic: 5.17 us -> 0 us
  Pallas kernels: 66.7 us -> 71.5 us
  local copies, waits for them, and re-layouts: 2.45 us -> 0 us
    convert_element_type x2 -> x0, other arithmetic: 5.17 us -> none  [the longest x1 4.13 us: shards(): first_sum.astype(jnp.float32)]
    pallas_call x0 -> x1, Pallas kernels: none -> 4.83 us  [shards(): pl.pallas_call(write_kernel, name='write_out', out_shape=(jax.ShapeDtypeS...]
    slice x2 -> x0, local copies, waits for them, and re-layouts: 2.45 us -> none  [the longest x1 1.27 us: shards(): small_sum[0, :hid]]
where the time goes in v3:
time: 73 us; the launch traced here: 72.8 us
  Pallas kernels  71.5 us (98%)
  between operations  1.29 us (2%)
    pallas_call x1, Pallas kernels, shards(): pl.pallas_call(lambda *refs: step_kernel(chips, spans, *refs), name='rank...  66.7 us
    pallas_call x1, Pallas kernels, shards(): pl.pallas_call(write_kernel, name='write_out', out_shape=(jax.ShapeDtypeS...  4.83 us

profile of v3, /device:TPU:0, one launch (start us, length us, event | category | flops | bytes accessed | tf_op | source)
XLA Modules:
  0.0 72.8 jit_solution(6428773655254267739)
XLA Ops:
  1.3 66.7 %rank_step.1 = (bf16[1024,1024]{1,0:T(8,128)(2,1)}, bf16[1024,256]{1,0:T(8,128)(2,1)}, f32[1,1152]{1,0:T(1,128)}) custom-call(s32[1]{0:T(128)S(6)} %copy.10.refs_0_, s32[1,256]{1,0:T(1,128)} %refs_1_.1, bf16[1,256,1024]{2,1,0:T(8,128)(2,1)} %refs_2_.1, bf16[1024,1024]{1,0:T(8,128)(2,1)} %refs_3_.1, f32[1,1024]{1,0:T(1,128)} %bitcast.3, bf16[1024,256]{1,0:T(8,128)(2,1)} %refs_5_.1), custom_call_target="tpu_custom_call" | custom-call | tf_op jit(solution)/shard_map/rank_step/pallas_call | solution.py:364
  68.0 4.8 %write_out.1 = (f32[1024,1024]{1,0:T(8,128)}, f32[1024,256]{1,0:T(8,128)}, f32[1,1024]{1,0:T(1,128)}, f32[1,1]{1,0:T(1,128)}) custom-call(bf16[1024,1024]{1,0:T(8,128)(2,1)} %get-tuple-element.11.first, bf16[1024,256]{1,0:T(8,128)(2,1)} %get-tuple-element.12.second, f32[1,1152]{1,0:T(1,128)} %get-tuple-element.13.small), custom_call_target="tpu_custom_call" | custom-call | tf_op jit(solution)/shard_map/write_out/pallas_call | solution.py:397

commit v4 on v3

--- a/solution.py
+++ b/solution.py
@@ -32,19 +32,19 @@
 
 
 class Reducer:
-    def __init__(self, place, chips, spans, read, result, small, small_out, scratch):
+    def __init__(self, place, chips, spans, grads, result, small, small_out, scratch):
         self.core, self.chip, self.span = place
         self.chips, self.spans = chips, spans
-        self.read, self.result = read, result
+        self.grads, self.result = grads, result
         self.small, self.small_out = small, small_out
         (
-            self.pair_buf, self.pair_in, self.half_sum, self.half_buf, self.chip_in,
+            self.pair_in, self.half_sum, self.half_buf, self.chip_in,
             self.block_sum, self.block_buf, self.span_in,
             self.small_pair, self.small_chip, self.small_span,
             self.pair_s, self.pair_r, self.chip_s, self.chip_r, self.span_s, self.span_r,
             self.small_s, self.small_r,
         ) = scratch
-        self.half = self.pair_buf.shape[1]
+        self.half = self.pair_in.shape[1]
         self.block = self.half // chips
         self.part = self.span_in.shape[2]
         self.owners = self.block // self.part
@@ -73,13 +73,13 @@
         return 2 * lax.rem(self.chip + k, self.chips) + self.core
 
     def pair_out(self, p):
-        self.pair_buf[p] = self.read(p, rows_at((1 - self.core) * self.half, self.half)).astype(jnp.bfloat16)
-        self.copy(("pair", p), self.pair_buf.at[p], self.pair_in.at[p], self.pair_s.at[0, p], self.pair_r.at[0, p], dp=self.partner())
+        away = self.grads.at[p, rows_at((1 - self.core) * self.half, self.half)]
+        self.copy(("pair", p), away, self.pair_in.at[p], self.pair_s.at[0, p], self.pair_r.at[0, p], dp=self.partner())
 
     def chip_out(self, p):
         self.settle(("pair", p))
-        own = self.read(p, rows_at(self.core * self.half, self.half))
-        total = own + self.pair_in[p].astype(jnp.float32)
+        own = self.grads[p, rows_at(self.core * self.half, self.half), :]
+        total = own + self.pair_in[p]
         self.half_sum[p] = total
         self.half_buf[p] = total.astype(jnp.bfloat16)
         for k in range(1, self.chips):
@@ -163,8 +163,7 @@
     part = block // owners_of(rows, chips, spans)
     vmem, dma = pltpu.VMEM, pltpu.SemaphoreType.DMA
     return [
-        vmem((pieces, half, width), jnp.bfloat16),
-        vmem((pieces, half, width), jnp.bfloat16),
+        vmem((pieces, half, width), jnp.float32),
         vmem((pieces, half, width), jnp.float32),
         vmem((pieces, half, width), jnp.bfloat16),
         vmem((pieces, chips - 1, block, width), jnp.bfloat16),
@@ -183,13 +182,12 @@
 
 def finish_reduce(red, pieces):
     stages = (red.span_out, red.span_back, red.chip_back, red.pair_back, lambda p: red.settle(("pair_back", p)))
-    smalls = {0: red.small_second, 1: red.small_third, 3: red.small_last}
-    for turn in range(pieces + len(stages) - 1):
-        for lag, stage in enumerate(stages):
-            if 0 <= turn - lag < pieces:
-                stage(turn - lag)
-        if turn in smalls:
-            smalls[turn]()
+    order = sorted((p + lag, n, p) for p in range(pieces) for n, lag in enumerate((0, 2.2, 4.3, 6.5, 9.0)))
+    smalls = {0: red.small_second, 3: red.small_third, 8: red.small_last}
+    for at, (_, n, p) in enumerate(order):
+        stages[n](p)
+        if at in smalls:
+            smalls[at]()
 
 
 def write_kernel(first, second, small, first_out, second_out, bias_out, loss_out, first_buf, second_buf, sem):
@@ -330,13 +328,10 @@
         total = total + dot(pair_grad.astype(jnp.bfloat16), keys[k], ((1,), (0,)))
     grad_emb = (total * pair_scale).astype(jnp.bfloat16)
 
-    def read(p, at):
-        return grads[p, at, :]
-
     def result(p, at):
         return second_out.at[at] if p == 0 else first_out.at[at, pl.ds((p - 1) * width, width)]
 
-    red = Reducer(place, chips, spans, read, result, lambda: small[...], small_out, scratch)
+    red = Reducer(place, chips, spans, grads, result, lambda: small[...], small_out, scratch)
     grads[0] = dot(hidden_t[...], grad_emb, ((1,), (0,)))
     red.pair_out(0)
     for p in range(1, pieces):

time: 73 us -> 71.9 us (0.985)
  Pallas kernels: 71.5 us -> 70.4 us
    pallas_call x1, Pallas kernels: 66.7 us -> 65.6 us  [shards(): pl.pallas_call(lambda *refs: step_kernel(chips, spans, *refs), name='rank...]
where the time goes in v4:
time: 71.9 us; the launch traced here: 71.7 us
  Pallas kernels  70.4 us (98%)
  between operations  1.29 us (2%)
    pallas_call x1, Pallas kernels, shards(): pl.pallas_call(lambda *refs: step_kernel(chips, spans, *refs), name='rank...  65.6 us
    pallas_call x1, Pallas kernels, shards(): pl.pallas_call(write_kernel, name='write_out', out_shape=(jax.ShapeDtypeS...  4.83 us

profile of v4, /device:TPU:0, one launch (start us, length us, event | category | flops | bytes accessed | tf_op | source)
XLA Modules:
  0.0 71.7 jit_solution(10330472777458042858)
XLA Ops:
  1.3 65.6 %rank_step.1 = (bf16[1024,1024]{1,0:T(8,128)(2,1)}, bf16[1024,256]{1,0:T(8,128)(2,1)}, f32[1,1152]{1,0:T(1,128)}) custom-call(s32[1]{0:T(128)S(6)} %copy.10.refs_0_, s32[1,256]{1,0:T(1,128)} %refs_1_.1, bf16[1,256,1024]{2,1,0:T(8,128)(2,1)} %refs_2_.1, bf16[1024,1024]{1,0:T(8,128)(2,1)} %refs_3_.1, f32[1,1024]{1,0:T(1,128)} %bitcast.3, bf16[1024,256]{1,0:T(8,128)(2,1)} %refs_5_.1), custom_call_target="tpu_custom_call" | custom-call | tf_op jit(solution)/shard_map/rank_step/pallas_call | solution.py:359
  66.9 4.8 %write_out.1 = (f32[1024,1024]{1,0:T(8,128)}, f32[1024,256]{1,0:T(8,128)}, f32[1,1024]{1,0:T(1,128)}, f32[1,1]{1,0:T(1,128)}) custom-call(bf16[1024,1024]{1,0:T(8,128)(2,1)} %get-tuple-element.11.first, bf16[1024,256]{1,0:T(8,128)(2,1)} %get-tuple-element.12.second, f32[1,1152]{1,0:T(1,128)} %get-tuple-element.13.small), custom_call_target="tpu_custom_call" | custom-call | tf_op jit(solution)/shard_map/write_out/pallas_call | solution.py:392

commit v5 on v4

--- a/solution.py
+++ b/solution.py
@@ -341,9 +341,11 @@
         small[:, cols] = jnp.sum(grad_pre.astype(jnp.float32), axis=0, keepdims=True)
         grads[p] = dot(feats_t[...], grad_pre, ((1,), (0,)))
         red.pair_out(p)
-        red.chip_out(p - 1)
+        if p > 1:
+            red.chip_out(p - 2)
     red.small_first()
-    red.chip_out(pieces - 1)
+    for p in range(max(pieces - 2, 0), pieces):
+        red.chip_out(p)
     finish_reduce(red, pieces)
 
 

time: 71.9 us -> 71.9 us (level)
  no operation moved by 1% of the time
where the time goes in v5:
time: 71.9 us; the launch traced here: 71.7 us
  Pallas kernels  70.4 us (98%)
  between operations  1.29 us (2%)
    pallas_call x1, Pallas kernels, shards(): pl.pallas_call(lambda *refs: step_kernel(chips, spans, *refs), name='rank...  65.6 us
    pallas_call x1, Pallas kernels, shards(): pl.pallas_call(write_kernel, name='write_out', out_shape=(jax.ShapeDtypeS...  4.83 us

profile of v5, /device:TPU:0, one launch (start us, length us, event | category | flops | bytes accessed | tf_op | source)
XLA Modules:
  0.0 71.7 jit_solution(17255098936679638177)
XLA Ops:
  1.3 65.6 %rank_step.1 = (bf16[1024,1024]{1,0:T(8,128)(2,1)}, bf16[1024,256]{1,0:T(8,128)(2,1)}, f32[1,1152]{1,0:T(1,128)}) custom-call(s32[1]{0:T(128)S(6)} %copy.10.refs_0_, s32[1,256]{1,0:T(1,128)} %refs_1_.1, bf16[1,256,1024]{2,1,0:T(8,128)(2,1)} %refs_2_.1, bf16[1024,1024]{1,0:T(8,128)(2,1)} %refs_3_.1, f32[1,1024]{1,0:T(1,128)} %bitcast.3, bf16[1024,256]{1,0:T(8,128)(2,1)} %refs_5_.1), custom_call_target="tpu_custom_call" | custom-call | tf_op jit(solution)/shard_map/rank_step/pallas_call | solution.py:361
  66.9 4.8 %write_out.1 = (f32[1024,1024]{1,0:T(8,128)}, f32[1024,256]{1,0:T(8,128)}, f32[1,1024]{1,0:T(1,128)}, f32[1,1]{1,0:T(1,128)}) custom-call(bf16[1024,1024]{1,0:T(8,128)(2,1)} %get-tuple-element.11.first, bf16[1024,256]{1,0:T(8,128)(2,1)} %get-tuple-element.12.second, f32[1,1152]{1,0:T(1,128)} %get-tuple-element.13.small), custom_call_target="tpu_custom_call" | custom-call | tf_op jit(solution)/shard_map/write_out/pallas_call | solution.py:394
